TPU v7x, 512 devices: a whole 4x4x16 slice. The times are simulated.
512 devices in a mesh: guide: 2 (over core), dp: 16 (over y, x), mp: 16 (over z).
Axes of the slice: x: 4, y: 4, z: 16, core: 2. Of those that a mesh axis runs over, the one named last changes fastest.
Arguments:
- states: bfloat16 [2, 128, 2048], P('guide', 'dp'), may hold values from -6 to 6
- lengths: int32 [2, 128], P('guide', 'dp'), may hold values from 1 to 32768, as said below
- sink_cache: bfloat16 [2, 128, 16, 2, 4, 128], P('guide', 'dp', 'mp'), may hold values from -48 to 48
- window_cache: bfloat16 [2, 128, 16, 2, 256, 128], P('guide', 'dp', 'mp'), may hold values from -360 to 360
- qkv_weight: bfloat16 [2048, 3, 16, 128], P(None, None, 'mp'), may hold values from -0.125 to 0.125
- out_weight: bfloat16 [16, 128, 2048], P('mp'), may hold values from -0.125 to 0.125
- expert_ids: int32 [2, 128, 8], replicated, may hold values from 0 to 63, all different within a row; in each aligned block of 8 rows (0 to 7, 8 to 15, ..., all dimensions but the last counted through in order) at most 2 rows name the same one
- route_weight: float32 [2, 128, 8], replicated, may hold values from 0.5 to 2
- expert_in: bfloat16 [2, 2048, 65536], P(None, None, ('guide', 'dp', 'mp')), may hold values from -0.125 to 0.125
- expert_out: bfloat16 [65536, 2048], P(('guide', 'dp', 'mp')), may hold values from -0.1875 to 0.1875
- vocab_weight: bfloat16 [2048, 26624], P(('guide', 'dp'), 'mp'), may hold values from -0.125 to 0.125
- guidance: float32 [128], P('dp'), may hold values from 1 to 5
Outputs:
- guided: float32 [128, 16, 2, 832], P('dp', 'mp', 'guide')
Inputs may be any that keep to these rules, and one draw needn't show every extreme that they name: `lengths`: one stream of one request has exactly 32768 cached positions. `expert_ids`: taking the tokens streams first, then requests, in aligned blocks of 8 tokens (the tokens of one device), no expert is named by more than 2 tokens of a block, a bound that some block reaches.
All inputs are finite; a program needn't handle non-finite values.
Results may differ from a plain program's by a relative error of at most 0.025.
Values may be sent and summed in bfloat16 or wider, within the bound.
A program may use at most 64 MiB of HBM per device.

v0:
```python
import math
import jax
import jax.numpy as jnp
from jax import lax
from jax.sharding import PartitionSpec as P

FFE = 1024
EPSILON = 1e-05


def partner(block, axis, stride):
    count = lax.axis_size(axis)
    route = []
    for low in range(count):
        high = low | 1 << stride
        if high != low and high < count:
            route += [(low, high), (high, low)]
    return lax.ppermute(block, axis, route)


def rms_norm(values):
    return values * lax.rsqrt(jnp.mean(values * values, axis=-1, keepdims=True) + EPSILON)


def rotate(vectors, positions):
    full_width = vectors.shape[-1]
    half_width = full_width // 2
    step_index = jnp.arange(half_width, dtype=jnp.float32)
    inverse = jnp.exp(step_index * (-2.0 * math.log(10000.0) / full_width))
    angles = positions.astype(jnp.float32)[:, None] * inverse[None, :]
    cosine = jnp.cos(angles)[:, None, :]
    sine_part = jnp.sin(angles)[:, None, :]
    first_half = vectors[..., :half_width]
    second = vectors[..., half_width:]
    return jnp.concatenate(
        [first_half * cosine - second * sine_part, second * cosine + first_half * sine_part],
        axis=-1,
    )


def body(
    states,
    lengths,
    sink_cache,
    window_cache,
    qkv_weight,
    out_weight,
    expert_ids,
    route_weight,
    expert_in,
    expert_out,
    vocab_weight,
    guidance,
):
    hidden = states[0]
    own_lengths = lengths[0]
    request_count = hidden.shape[0]
    normed = rms_norm(hidden.astype(jnp.float32)).astype(jnp.bfloat16)
    projected = jnp.einsum("rd,dthe->rthe", normed, qkv_weight, preferred_element_type=jnp.float32)
    query_rot = rotate(projected[:, 0], own_lengths).astype(jnp.bfloat16)
    fresh_key = rotate(projected[:, 1], own_lengths).astype(jnp.bfloat16)
    fresh_value = projected[:, 2].astype(jnp.bfloat16)
    sink_rows = sink_cache[0]
    window_rows = window_cache[0]
    sink_count = sink_rows.shape[3]
    window_count = window_rows.shape[3]
    root_size = math.sqrt(query_rot.shape[-1])
    sink_scores = (
        jnp.einsum(
            "rhe,rhse->rhs", query_rot, sink_rows[:, :, 0], preferred_element_type=jnp.float32
        )
        / root_size
    )
    window_scores = (
        jnp.einsum(
            "rhe,rhwe->rhw", query_rot, window_rows[:, :, 0], preferred_element_type=jnp.float32
        )
        / root_size
    )
    self_scores = (
        jnp.einsum("rhe,rhe->rh", query_rot, fresh_key, preferred_element_type=jnp.float32)
        / root_size
    )
    length_limit = own_lengths[:, None, None]
    sink_valid = jnp.arange(sink_count, dtype=jnp.int32)[None, None, :] < length_limit
    window_valid = (
        jnp.arange(window_count, dtype=jnp.int32)[None, None, :]
        >= sink_count + window_count - length_limit
    )
    sink_scores = jnp.where(sink_valid, sink_scores, -1e30)
    window_scores = jnp.where(window_valid, window_scores, -1e30)
    highest = jnp.maximum(
        jnp.maximum(jnp.max(sink_scores, axis=-1), jnp.max(window_scores, axis=-1)), self_scores
    )
    sink_exp = jnp.exp(sink_scores - highest[..., None])
    window_exp = jnp.exp(window_scores - highest[..., None])
    self_exp = jnp.exp(self_scores - highest)
    totals = jnp.sum(sink_exp, axis=-1) + jnp.sum(window_exp, axis=-1) + self_exp
    sink_prob = (sink_exp / totals[..., None]).astype(jnp.bfloat16)
    window_prob = (window_exp / totals[..., None]).astype(jnp.bfloat16)
    self_prob = (self_exp / totals).astype(jnp.bfloat16)
    mixture = (
        jnp.einsum(
            "rhs,rhse->rhe", sink_prob, sink_rows[:, :, 1], preferred_element_type=jnp.float32
        )
        + jnp.einsum(
            "rhw,rhwe->rhe", window_prob, window_rows[:, :, 1], preferred_element_type=jnp.float32
        )
        + self_prob[..., None].astype(jnp.float32) * fresh_value.astype(jnp.float32)
    ).astype(jnp.bfloat16)
    partial_out = jnp.einsum("rhe,hed->rd", mixture, out_weight, preferred_element_type=jnp.float32)
    attention_out = lax.psum(partial_out, "mp")
    residual = (hidden.astype(jnp.float32) + attention_out).astype(jnp.bfloat16)
    moe_in = rms_norm(residual.astype(jnp.float32)).astype(jnp.bfloat16)
    unit_count = expert_in.shape[2]
    unit_start = lax.axis_index(("guide", "dp", "mp")) * unit_count
    unit_expert = (unit_start + jnp.arange(unit_count, dtype=jnp.int32)) // FFE
    choice_rows = expert_ids.reshape(-1, expert_ids.shape[-1])
    route_rows = route_weight.reshape(-1, route_weight.shape[-1])
    coefficient = jnp.sum(
        jnp.where(
            choice_rows[:, :, None] == unit_expert[None, None, :], route_rows[:, :, None], 0.0
        ),
        axis=1,
    )
    piece = lax.all_gather(moe_in, ("guide", "dp"), axis=0, tiled=True)
    gate = jnp.dot(piece, expert_in[0], preferred_element_type=jnp.float32)
    upward = jnp.dot(piece, expert_in[1], preferred_element_type=jnp.float32)
    activated = (jax.nn.silu(gate) * upward * coefficient).astype(jnp.bfloat16)
    expert_terms = jnp.dot(activated, expert_out, preferred_element_type=jnp.float32)
    expert_part = lax.psum_scatter(expert_terms, ("guide", "dp"), scatter_dimension=0, tiled=True)
    expert_total = lax.psum(expert_part, "mp")
    final = rms_norm(residual.astype(jnp.float32) + expert_total).astype(jnp.bfloat16)
    final_all = lax.all_gather(final, ("guide", "dp"), axis=0, tiled=True)
    row_share = vocab_weight.shape[0]
    share_start = lax.axis_index(("guide", "dp")) * row_share
    final_cols = lax.dynamic_slice_in_dim(final_all, share_start, row_share, 1)
    logits = lax.psum_scatter(
        jnp.dot(final_cols, vocab_weight, preferred_element_type=jnp.float32).astype(jnp.bfloat16),
        ("guide", "dp"),
        scatter_dimension=0,
        tiled=True,
    ).astype(jnp.float32)
    half_width = logits.shape[1] // 2
    stream_index = lax.axis_index("guide")
    own_half = lax.dynamic_slice_in_dim(logits, stream_index * half_width, half_width, 1)
    other_half = lax.dynamic_slice_in_dim(logits, (1 - stream_index) * half_width, half_width, 1)
    partner_logits = partner(other_half, "guide", 0)
    is_conditional = stream_index == 0
    conditional = jnp.where(is_conditional, own_half, partner_logits)
    unconditional = jnp.where(is_conditional, partner_logits, own_half)
    guided = unconditional + guidance[:, None] * (conditional - unconditional)
    return guided.reshape(request_count, 1, 1, half_width)


def solution(mesh):
    in_specs = (
        P("guide", "dp", None),
        P("guide", "dp"),
        P("guide", "dp", "mp", None, None, None),
        P("guide", "dp", "mp", None, None, None),
        P(None, None, "mp", None),
        P("mp", None, None),
        P(),
        P(),
        P(None, None, ("guide", "dp", "mp")),
        P(("guide", "dp", "mp"), None),
        P(("guide", "dp"), "mp"),
        P("dp"),
    )
    out_specs = P("dp", "mp", "guide", None)
    return jax.shard_map(body, mesh=mesh, in_specs=in_specs, out_specs=out_specs, check_vma=False)
```

profile of v0, /device:TPU:1, one launch (start us, length us, event | category | flops | bytes accessed | tf_op | source)
XLA Modules:
  0.0 657.1 jit_solution(2036525778644055514)
XLA Ops:
  6.6 0.8 bitcast_convert_fusion
  7.4 0.8 broadcast_subtract_fusion
  8.2 0.9 fusion.23
  9.1 1.2 fusion
  10.5 0.2 fusion.6
  10.7 0.1 fusion.35
  10.9 0.2 fusion.57
  11.1 0.2 fusion.46
  11.4 0.2 fusion.37
  11.7 0.2 fusion.5
  12.0 0.1 fusion.36
  12.1 0.9 fusion.11
  13.0 128.0 %all-reduce.5.cloned.1.call-done = f32[8,2048]{1,0:T(8,128)} async-done(((f32[8,2048]{1,0:T(8,128)}), f32[8,2048]{1,0:T(8,128)}) %all-reduce.5.cloned.1.call-update) | async-done | bytes 65552 | tf_op jit(solution)/shard_map/psum | solution.py:112
  141.0 1.0 fusion.26
  142.0 0.7 fusion.27
  142.8 0.1 copy.24
  143.1 1.3 select_reduce_fusion
  144.4 65.6 %all-gather.3.cloned.1.call-done = bf16[256,2048]{1,0:T(8,128)(2,1)} async-done(((bf16[8,2048]{1,0:T(8,128)(2,1)}), bf16[256,2048]{1,0:T(8,128)(2,1)}) %all-gather.3.cloned.1.call-update) | async-done | bytes 1048592 | tf_op jit(solution)/shard_map/all_gather | solution.py:126
  210.0 1.9 fusion.9
  211.9 3.2 fusion.4
  215.2 99.4 %reduce-scatter.2.cloned.1.call-done = f32[8,2048]{1,0:T(8,128)} async-done(((f32[256,2048]{1,0:T(8,128)}), f32[8,2048]{1,0:T(8,128)}) %reduce-scatter.2.cloned.1.call-update) | async-done | bytes 65552 | tf_op jit(solution)/shard_map/reduce_scatter | solution.py:131
  314.6 125.9 %all-reduce.7.cloned.1.call-done = f32[8,2048]{1,0:T(8,128)} async-done(((f32[8,2048]{1,0:T(8,128)}), f32[8,2048]{1,0:T(8,128)}) %all-reduce.7.cloned.1.call-update) | async-done | bytes 65552 | tf_op jit(solution)/shard_map/psum | solution.py:132
  440.5 1.0 multiply_reduce_fusion
  441.5 1.5 multiply_convert_fusion
  443.1 65.8 %all-gather.5.cloned.1.call-done = bf16[256,2048]{1,0:T(8,128)(2,1)} async-done(((bf16[8,2048]{1,0:T(8,128)(2,1)}), bf16[256,2048]{1,0:T(8,128)(2,1)}) %all-gather.5.cloned.1.call-update) | async-done | bytes 1048592 | tf_op jit(solution)/shard_map/all_gather | solution.py:134
  508.9 2.2 convolution_convert_fusion
  511.1 1.3 dynamic-slice
  513.1 132.5 %all-reduce.9.cloned.1.call-done = bf16[256,1664]{1,0:T(8,128)(2,1)} async-done(((bf16[256,1664]{1,0:T(8,128)(2,1)}), bf16[256,1664]{1,0:T(8,128)(2,1)}) %all-reduce.9.cloned.1.call-update) | async-done | bytes 851984
  645.6 0.7 dynamic-slice_convert_fusion
  646.4 2.3 collective-permute-start
  648.7 0.8 collective-permute-done
  649.6 0.6 copy.26
  (56 shorter events, 1.3 us)
Async XLA Ops:
  6.5 2.5 copy-start
  6.5 4.8 copy-start.9
  6.5 3.9 copy-start.5
  6.5 4.2 copy-start.11
  6.5 5.6 copy-start.3
  6.5 134.5 %all-reduce.5.cloned.1.call-start = ((), (), s32[]{:S(2)}) async-start(), calls=%async_computation.1 | async-start | bytes 131072 | tf_op jit(solution)/shard_map/psum | solution.py:112
  9.1 131.9 %copy-start.4 = (bf16[1,8,2048]{2,1,0:T(8,128)(2,1)S(1)}, bf16[1,8,2048]{2,1,0:T(8,128)(2,1)}, u32[]{:S(2)}) copy-start(bf16[1,8,2048]{2,1,0:T(8,128)(2,1)} %param.12) | copy-start | bytes 98308
  9.1 133.7 %copy-start.7 = (s32[2,128,8]{1,2,0:T(8,128)S(1)}, s32[2,128,8]{1,2,0:T(8,128)}, u32[]{:S(2)}) copy-start(s32[2,128,8]{1,2,0:T(8,128)} %param.18) | copy-start | bytes 24580
  10.3 132.6 %copy-start.8 = (f32[2,128,8]{1,2,0:T(8,128)S(1)}, f32[2,128,8]{1,2,0:T(8,128)}, u32[]{:S(2)}) copy-start(f32[2,128,8]{1,2,0:T(8,128)} %param.19) | copy-start | bytes 24580
  12.1 199.8 %copy-start.2 = (bf16[128,2048]{1,0:T(8,128)(2,1)S(1)}, bf16[128,2048]{1,0:T(8,128)(2,1)}, u32[]{:S(2)}) copy-start(bf16[128,2048]{1,0:T(8,128)(2,1)} %param.21) | copy-start | bytes 1572868
  13.0 197.0 %all-gather.3.cloned.1.call-start = ((), (), s32[]{:S(2)}) async-start(), calls=%async_computation.2 | async-start | bytes 1081344 | tf_op jit(solution)/shard_map/all_gather | solution.py:126
  142.7 171.9 %reduce-scatter.2.cloned.1.call-start = ((), (), s32[]{:S(2)}) async-start(), calls=%async_computation.3 | async-start | bytes 2162688 | tf_op jit(solution)/shard_map/reduce_scatter | solution.py:131
  210.0 1.9 copy-start.1
  215.1 293.8 %copy-start.6 = (bf16[64,1664]{1,0:T(8,128)(2,1)S(1)}, bf16[64,1664]{1,0:T(8,128)(2,1)}, u32[]{:S(2)}) copy-start(bf16[64,1664]{1,0:T(8,128)(2,1)} %param.22) | copy-start | bytes 638980
  215.1 434.4 %copy-start.10 = (f32[8]{0:T(128)S(1)}, f32[8]{0:T(128)}, u32[]{:S(2)}) copy-start(f32[8]{0:T(128)} %param.23) | copy-start | bytes 100
  215.1 225.4 %all-reduce.7.cloned.1.call-start = ((), (), s32[]{:S(2)}) async-start(), calls=%async_computation.4 | async-start | bytes 131072 | tf_op jit(solution)/shard_map/psum | solution.py:132
  314.6 194.3 %all-gather.5.cloned.1.call-start = ((), (), s32[]{:S(2)}) async-start(), calls=%async_computation.5 | async-start | bytes 1081344 | tf_op jit(solution)/shard_map/all_gather | solution.py:134
  443.1 202.6 %all-reduce.9.cloned.1.call-start = ((), (), s32[]{:S(2)}) async-start(), calls=%async_computation.6 | async-start | bytes 1703936
  646.4 3.1 collective-permute-start
Sparse Core Ops, SparseCore 0:
  13.1 127.8 all-reduce.4
  144.7 65.3 all-gather.2
  215.3 99.2 reduce-scatter.1
  316.9 123.6 all-reduce.6
  443.6 65.3 all-gather.4
  512.1 133.5 all-reduce.8
where the time goes:
time: 658 us; the launch traced here: 657 us
  waiting for transfers between devices  618 us (94%)
  between operations  14.4 us (2%)
  matrix products  9.92 us (2%)
  other arithmetic  9.7 us (1%)
    unnamed x7, waiting for transfers between devices  133 us
    psum x1, waiting for transfers between devices, body(): attention_out = lax.psum(partial_out, 'mp')  128 us
    psum x1, waiting for transfers between devices, body(): expert_total = lax.psum(expert_part, 'mp')  126 us
    reduce_scatter x1, waiting for transfers between devices, body(): lax.psum_scatter(expert_terms, ('guide', 'dp'), scatter_dimension=0, tile...  99.4 us
    all_gather x1, waiting for transfers between devices, body(): final_all = lax.all_gather(final, ('guide', 'dp'), axis=0, tiled=True)  65.8 us
    all_gather x1, waiting for transfers between devices, body(): piece = lax.all_gather(moe_in, ('guide', 'dp'), axis=0, tiled=True)  65.6 us
  transfers between devices with their start and end apart: 7, of which 7 were waited for; matrix products, arithmetic and copies ran while one was open for 0% of the time, Pallas kernels for 0%

commit v1 on v0

--- a/solution.py
+++ b/solution.py
@@ -109,7 +109,8 @@
         + self_prob[..., None].astype(jnp.float32) * fresh_value.astype(jnp.float32)
     ).astype(jnp.bfloat16)
     partial_out = jnp.einsum("rhe,hed->rd", mixture, out_weight, preferred_element_type=jnp.float32)
-    attention_out = lax.psum(partial_out, "mp")
+    terms = lax.all_gather(partial_out, "mp", axis=0, tiled=False)
+    attention_out = terms.sum(axis=0)
     residual = (hidden.astype(jnp.float32) + attention_out).astype(jnp.bfloat16)
     moe_in = rms_norm(residual.astype(jnp.float32)).astype(jnp.bfloat16)
     unit_count = expert_in.shape[2]

time: 658 us -> 596 us (0.906)
  waiting for transfers between devices: 618 us -> 556 us
    psum x1 -> x0, waiting for transfers between devices: 128 us -> none  [body(): attention_out = lax.psum(partial_out, 'mp')]
    all_gather x0 -> x1, waiting for transfers between devices: none -> 67 us  [body(): terms = lax.all_gather(partial_out, 'mp', axis=0, tiled=False)]
where the time goes in v1:
time: 596 us
  waiting for transfers between devices  556 us (93%)
  between operations  14.3 us (2%)
  other arithmetic  10.1 us (2%)
  matrix products  9.87 us (2%)
    unnamed x7, waiting for transfers between devices  133 us
    psum x1, waiting for transfers between devices, body(): expert_total = lax.psum(expert_part, 'mp')  126 us
    reduce_scatter x1, waiting for transfers between devices, body(): lax.psum_scatter(expert_terms, ('guide', 'dp'), scatter_dimension=0, tile...  99.3 us
    all_gather x1, waiting for transfers between devices, body(): terms = lax.all_gather(partial_out, 'mp', axis=0, tiled=False)  67 us
    all_gather x1, waiting for transfers between devices, body(): final_all = lax.all_gather(final, ('guide', 'dp'), axis=0, tiled=True)  66.3 us
    all_gather x1, waiting for transfers between devices, body(): piece = lax.all_gather(moe_in, ('guide', 'dp'), axis=0, tiled=True)  64.2 us
  transfers between devices with their start and end apart: 7, of which 7 were waited for; matrix products, arithmetic and copies ran while one was open for 0% of the time, Pallas kernels for 0%

profile of v1, /device:TPU:1, one launch (start us, length us, event | category | flops | bytes accessed | tf_op | source)
XLA Modules:
  0.0 595.8 jit_solution(16228075824114601059)
XLA Ops:
  6.6 0.8 bitcast_convert_fusion
  7.4 0.8 broadcast_subtract_fusion
  8.2 0.9 fusion.23
  9.1 1.1 fusion
  10.4 0.2 fusion.6
  10.7 0.1 fusion.35
  10.9 0.2 fusion.57
  11.1 0.2 fusion.46
  11.3 0.2 fusion.37
  11.6 0.2 fusion.5
  11.9 0.1 fusion.36
  12.0 0.9 fusion.11
  13.0 67.0 %all-gather.9.cloned.1.call-done = f32[128,2048]{1,0:T(8,128)} async-done(((f32[8,2048]{1,0:T(8,128)}), f32[128,2048]{1,0:T(8,128)}) %all-gather.9.cloned.1.call-update) | async-done | bytes 1048592 | tf_op jit(solution)/shard_map/all_gather | solution.py:112
  80.0 1.3 bitcast_reduce_fusion
  81.3 0.1 fusion.26
  81.4 0.7 fusion.27
  82.5 1.3 select_reduce_fusion
  83.8 64.2 %all-gather.5.cloned.1.call-done = bf16[256,2048]{1,0:T(8,128)(2,1)} async-done(((bf16[8,2048]{1,0:T(8,128)(2,1)}), bf16[256,2048]{1,0:T(8,128)(2,1)}) %all-gather.5.cloned.1.call-update) | async-done | bytes 1048592 | tf_op jit(solution)/shard_map/all_gather | solution.py:127
  148.0 1.9 fusion.9
  149.9 3.2 fusion.4
  153.2 99.3 %reduce-scatter.2.cloned.1.call-done = f32[8,2048]{1,0:T(8,128)} async-done(((f32[256,2048]{1,0:T(8,128)}), f32[8,2048]{1,0:T(8,128)}) %reduce-scatter.2.cloned.1.call-update) | async-done | bytes 65552 | tf_op jit(solution)/shard_map/reduce_scatter | solution.py:132
  252.6 125.8 %all-reduce.4.cloned.1.call-done = f32[8,2048]{1,0:T(8,128)} async-done(((f32[8,2048]{1,0:T(8,128)}), f32[8,2048]{1,0:T(8,128)}) %all-reduce.4.cloned.1.call-update) | async-done | bytes 65552 | tf_op jit(solution)/shard_map/psum | solution.py:133
  378.4 1.0 multiply_reduce_fusion
  379.4 1.5 multiply_convert_fusion
  381.0 66.3 %all-gather.7.cloned.1.call-done = bf16[256,2048]{1,0:T(8,128)(2,1)} async-done(((bf16[8,2048]{1,0:T(8,128)(2,1)}), bf16[256,2048]{1,0:T(8,128)(2,1)}) %all-gather.7.cloned.1.call-update) | async-done | bytes 1048592 | tf_op jit(solution)/shard_map/all_gather | solution.py:135
  447.3 2.2 convolution_convert_fusion
  449.5 1.3 dynamic-slice
  451.4 132.9 %all-reduce.6.cloned.1.call-done = bf16[256,1664]{1,0:T(8,128)(2,1)} async-done(((bf16[256,1664]{1,0:T(8,128)(2,1)}), bf16[256,1664]{1,0:T(8,128)(2,1)}) %all-reduce.6.cloned.1.call-update) | async-done | bytes 851984
  584.3 0.7 dynamic-slice_convert_fusion
  585.1 2.3 collective-permute-start
  587.4 0.8 collective-permute-done
  588.3 0.6 copy.26
  (57 shorter events, 1.4 us)
Async XLA Ops:
  6.5 2.5 copy-start
  6.5 4.7 copy-start.9
  6.5 3.9 copy-start.5
  6.5 4.1 copy-start.11
  6.5 5.5 copy-start.3
  6.5 73.4 %all-gather.9.cloned.1.call-start = ((), (), s32[]{:S(2)}) async-start(), calls=%async_computation.5 | async-start | bytes 1114112 | tf_op jit(solution)/shard_map/all_gather | solution.py:112
  10.2 71.0 %copy-start.4 = (bf16[1,8,2048]{2,1,0:T(8,128)(2,1)S(1)}, bf16[1,8,2048]{2,1,0:T(8,128)(2,1)}, u32[]{:S(2)}) copy-start(bf16[1,8,2048]{2,1,0:T(8,128)(2,1)} %param.12) | copy-start | bytes 98308
  10.4 71.8 %copy-start.7 = (s32[2,128,8]{1,2,0:T(8,128)S(1)}, s32[2,128,8]{1,2,0:T(8,128)}, u32[]{:S(2)}) copy-start(s32[2,128,8]{1,2,0:T(8,128)} %param.18) | copy-start | bytes 24580
  10.6 71.7 %copy-start.8 = (f32[2,128,8]{1,2,0:T(8,128)S(1)}, f32[2,128,8]{1,2,0:T(8,128)}, u32[]{:S(2)}) copy-start(f32[2,128,8]{1,2,0:T(8,128)} %param.19) | copy-start | bytes 24580
  12.9 135.1 %all-gather.5.cloned.1.call-start = ((), (), s32[]{:S(2)}) async-start(), calls=%async_computation.1 | async-start | bytes 1081344 | tf_op jit(solution)/shard_map/all_gather | solution.py:127
  81.2 68.6 %copy-start.2 = (bf16[128,2048]{1,0:T(8,128)(2,1)S(1)}, bf16[128,2048]{1,0:T(8,128)(2,1)}, u32[]{:S(2)}) copy-start(bf16[128,2048]{1,0:T(8,128)(2,1)} %param.21) | copy-start | bytes 1572868
  82.1 170.4 %reduce-scatter.2.cloned.1.call-start = ((), (), s32[]{:S(2)}) async-start(), calls=%async_computation.2 | async-start | bytes 2162688 | tf_op jit(solution)/shard_map/reduce_scatter | solution.py:132
  148.0 1.9 copy-start.1
  153.1 294.2 %copy-start.6 = (bf16[64,1664]{1,0:T(8,128)(2,1)S(1)}, bf16[64,1664]{1,0:T(8,128)(2,1)}, u32[]{:S(2)}) copy-start(bf16[64,1664]{1,0:T(8,128)(2,1)} %param.22) | copy-start | bytes 638980
  153.1 435.1 %copy-start.10 = (f32[8]{0:T(128)S(1)}, f32[8]{0:T(128)}, u32[]{:S(2)}) copy-start(f32[8]{0:T(128)} %param.23) | copy-start | bytes 100
  153.1 225.3 %all-reduce.4.cloned.1.call-start = ((), (), s32[]{:S(2)}) async-start(), calls=%async_computation.3 | async-start | bytes 131072 | tf_op jit(solution)/shard_map/psum | solution.py:133
  252.5 194.7 %all-gather.7.cloned.1.call-start = ((), (), s32[]{:S(2)}) async-start(), calls=%async_computation.4 | async-start | bytes 1081344 | tf_op jit(solution)/shard_map/all_gather | solution.py:135
  380.9 203.4 %all-reduce.6.cloned.1.call-start = ((), (), s32[]{:S(2)}) async-start(), calls=%async_computation.6 | async-start | bytes 1703936
  585.1 3.1 collective-permute-start
Sparse Core Ops, SparseCore 0:
  13.0 66.8 all-gather.8
  83.1 64.8 all-gather.4
  153.2 99.2 reduce-scatter.1
  254.7 123.6 all-reduce.3
  381.9 65.3 all-gather.6
  450.8 133.5 all-reduce.5
